TPU v7x, 32 devices: a whole 2x2x4 slice. The times are simulated.
32 devices in a mesh: parts: 2 (over y), expert: 8 (over z, x), group: 1, tensor: 2 (over core).
Axes of the slice: x: 2, y: 2, z: 4, core: 2. Of those that a mesh axis runs over, the one named last changes fastest.
Arguments:
- hidden_in: bfloat16 [3, 64, 4096], P(None, ('parts', 'expert', 'group')), parts along dimension 1, may hold values from -6 to 6
- queries: bfloat16 [3, 64, 32, 128], P(None, ('parts', 'expert', 'group'), 'tensor'), parts along dimension 1, may hold values from -32 to 32
- new_keys: bfloat16 [3, 64, 4, 128], P(None, ('parts', 'expert', 'group'), 'tensor'), parts along dimension 1, may hold values from -4 to 4
- new_values: bfloat16 [3, 64, 4, 128], P(None, ('parts', 'expert', 'group'), 'tensor'), parts along dimension 1, may hold values from -8 to 8
- cache_keys: bfloat16 [64, 4, 128, 128], P(('parts', 'expert', 'group'), 'tensor'), parts along dimension 0, may hold values from -4 to 4
- cache_values: bfloat16 [64, 4, 128, 128], P(('parts', 'expert', 'group'), 'tensor'), parts along dimension 0, may hold values from -8 to 8
- route_ids: int32 [3, 64, 8], P(None, ('parts', 'expert', 'group')), parts along dimension 1, may hold values from 0 to 15, all different within a row; in each aligned block of 4 rows (0 to 3, 4 to 7, ..., all dimensions but the last counted through in order) at most 4 rows name the same one
- route_weights: float32 [3, 64, 8], P(None, ('parts', 'expert', 'group')), parts along dimension 1, may hold values from 0.1 to 1
- norm_gain: float32 [4096], replicated, may hold values from 0.25 to 1.75
- gate_weight: bfloat16 [16, 4096, 768], P('expert', 'group', 'tensor'), may hold values from -0.09375 to 0.09375
- up_weight: bfloat16 [16, 4096, 768], P('expert', 'group', 'tensor'), may hold values from -0.09375 to 0.09375
- down_weight: bfloat16 [16, 768, 4096], P('expert', None, ('group', 'tensor')), may hold values from -0.21875 to 0.21875
- ancestor_counts: int32 [64], P(('parts', 'expert', 'group')), parts along dimension 0, may hold values from 0 to 5, as said below
Outputs:
- layer_out: bfloat16 [3, 64, 4096], P(None, ('parts', 'expert', 'group')), parts along dimension 1
- resampled_keys: bfloat16 [64, 4, 131, 128], P(('parts', 'expert', 'group'), 'tensor'), parts along dimension 0
- resampled_values: bfloat16 [64, 4, 131, 128], P(('parts', 'expert', 'group'), 'tensor'), parts along dimension 0
There are 2 independent parts, one for each index of `parts`. A program takes and returns all parts, laid end to end along the dimension named above; an argument that names none is the same for every part. Nothing has to cross between parts.
Inputs may be any that keep to these rules, and one draw needn't show every extreme that they name: `route_ids`: each row names 8 different experts; in each aligned block of 4 rows (the rows of one device in one step) no expert is named by more than 4 rows. `ancestor_counts`: the counts sum to 32, and every particle i descends from a particle within 2 positions of i.
All inputs are finite; a program needn't handle non-finite values.
Results may differ from a plain program's by a relative error of at most 0.0075.
Values may be sent and summed in bfloat16 or wider, within the bound.
A program may use at most 64 MiB of HBM per device.

v0:
```python
import math
import jax
import jax.numpy as jnp
from jax import lax
from jax.sharding import PartitionSpec as P

REACH = 2
epsilon = 1e-06
highest = lax.Precision.HIGHEST


def padded(cells, sides, width):
    for axis, dim in sides:
        count = lax.axis_size(axis)
        ends = count - 1
        head = lax.slice_in_dim(cells, 0, width, axis=dim)
        tail = lax.slice_in_dim(cells, cells.shape[dim] - width, cells.shape[dim], axis=dim)
        cells = jnp.concatenate(
            [
                lax.ppermute(tail, axis, [(i, (i + 1) % count) for i in range(ends)]),
                cells,
                lax.ppermute(head, axis, [((i + 1) % count, i) for i in range(ends)]),
            ],
            axis=dim,
        )
    return cells


def grouped_shards(
    hidden_in,
    queries,
    new_keys,
    new_values,
    cache_keys,
    cache_values,
    route_ids,
    route_weights,
    norm_gain,
    gate_weight,
    up_weight,
    down_weight,
    ancestor_counts,
):
    step_count, token_count, query_heads, head_width = queries.shape
    key_heads = cache_keys.shape[1]
    cached = cache_keys.shape[2]
    group_size = query_heads // key_heads
    cache_pair = jnp.stack([cache_keys, cache_values])
    fresh_pair = jnp.transpose(jnp.stack([new_keys, new_values]), (0, 2, 3, 1, 4))
    both_kv = jnp.concatenate([cache_pair, fresh_pair], axis=3)
    length = both_kv.shape[3]
    grouped = queries.reshape(step_count, token_count, key_heads, group_size, head_width)
    scores = jnp.einsum(
        "sphgd,phld->sphgl", grouped, both_kv[0], preferred_element_type=jnp.float32
    ) / math.sqrt(head_width)
    allowed = lax.broadcasted_iota(
        jnp.int32, (step_count, length), 1
    ) <= cached + lax.broadcasted_iota(jnp.int32, (step_count, length), 0)
    scores = jnp.where(allowed[:, None, None, None, :], scores, -1e30)
    exponent = jnp.exp(scores - jnp.max(scores, axis=-1, keepdims=True))
    attn_weights = (exponent / jnp.sum(exponent, axis=-1, keepdims=True)).astype(jnp.bfloat16)
    attended = jnp.einsum(
        "sphgl,phld->sphgd", attn_weights, both_kv[1], preferred_element_type=jnp.float32
    )
    attended = attended.astype(jnp.bfloat16).reshape(
        step_count, token_count, query_heads * head_width
    )
    attended = lax.all_gather(attended, "tensor", axis=2, tiled=True)
    expert_count = lax.axis_size("expert")
    group_count = lax.axis_size("group")
    tensor_count = lax.axis_size("tensor")
    tensor_index = lax.axis_index("tensor")
    expert_local = gate_weight.shape[0]
    experts_all = expert_local * expert_count
    chosen_count = route_ids.shape[2]
    model_width = hidden_in.shape[2]
    column_width = down_weight.shape[2]
    capacity = min(token_count, max(2, 2 * token_count * chosen_count // experts_all))
    pair_count = token_count * chosen_count
    expert_iota = jnp.arange(experts_all, dtype=jnp.int32)
    slot_iota = jnp.arange(capacity, dtype=jnp.int32)
    token_owner = (
        (jnp.arange(pair_count) // chosen_count)[:, None] == jnp.arange(token_count)[None, :]
    ).astype(jnp.float32)
    halves = []
    for step_index in range(step_count):
        residual = hidden_in[step_index].astype(jnp.float32) + attended[step_index].astype(
            jnp.float32
        )
        normed = (
            residual
            * lax.rsqrt(jnp.mean(residual * residual, axis=-1, keepdims=True) + epsilon)
            * norm_gain
        ).astype(jnp.bfloat16)
        chosen = route_ids[step_index].reshape(pair_count)
        route_share = route_weights[step_index] / jnp.sum(
            route_weights[step_index], axis=-1, keepdims=True
        )
        expert_hits = (chosen[:, None] == expert_iota[None, :]).astype(jnp.int32)
        position = jnp.sum((jnp.cumsum(expert_hits, axis=0) - expert_hits) * expert_hits, axis=1)
        slotted = (
            expert_hits[:, :, None]
            * (position[:, None, None] == slot_iota[None, None, :]).astype(jnp.int32)
        ).astype(jnp.float32)
        dispatch = jnp.einsum("rec,rt->ect", slotted, token_owner, precision=highest)
        dispatch = dispatch.reshape(expert_count, expert_local, capacity, token_count).astype(
            jnp.bfloat16
        )
        combine = jnp.einsum(
            "rec,rt,r->tec",
            slotted,
            token_owner,
            route_share.reshape(pair_count),
            precision=highest,
        )
        combine = combine.reshape(token_count, expert_count, expert_local, capacity)
        feature_blocks = normed.reshape(token_count, group_count, model_width // group_count)
        outgoing = jnp.einsum(
            "aict,tgd->agicd", dispatch, feature_blocks, preferred_element_type=jnp.float32
        ).astype(jnp.bfloat16)
        flattened = outgoing.reshape(
            expert_count * group_count, expert_local, capacity, model_width // group_count
        )
        received = lax.all_to_all(
            flattened, ("expert", "group"), split_axis=0, concat_axis=0, tiled=True
        )
        gate_part = jnp.einsum(
            "seki,eif->sekf", received, gate_weight, preferred_element_type=jnp.float32
        ).astype(jnp.bfloat16)
        up_part = jnp.einsum(
            "seki,eif->sekf", received, up_weight, preferred_element_type=jnp.float32
        ).astype(jnp.bfloat16)
        gate_sum = lax.psum(gate_part, "group").astype(jnp.float32)
        up_sum = lax.psum(up_part, "group").astype(jnp.float32)
        hidden = (jax.nn.silu(gate_sum) * up_sum).astype(jnp.bfloat16)
        hidden = lax.all_gather(hidden, "tensor", axis=3, tiled=True)
        answered = jnp.einsum(
            "sekf,efo->seko", hidden, down_weight, preferred_element_type=jnp.float32
        ).astype(jnp.bfloat16)
        returned = lax.all_to_all(
            answered, ("expert", "group"), split_axis=0, concat_axis=0, tiled=True
        )
        returned = returned.reshape(
            expert_count, group_count, expert_local, capacity, column_width
        ).astype(jnp.float32)
        expert_mix = jnp.einsum("taic,agicd->tgd", combine, returned, precision=highest)
        own_columns = lax.dynamic_index_in_dim(
            residual.reshape(token_count, group_count, tensor_count, column_width),
            tensor_index,
            2,
            keepdims=False,
        )
        halves.append((own_columns + expert_mix).astype(jnp.bfloat16))
    stacked = jnp.stack(halves)
    layer_out = lax.all_gather(stacked, "tensor", axis=3, tiled=True).reshape(
        step_count, token_count, model_width
    )
    every_count = lax.all_gather(ancestor_counts, ("expert", "group"), axis=0, tiled=True)
    running = jnp.cumsum(every_count)
    first_index = lax.axis_index(("expert", "group")) * token_count
    own_index = first_index + jnp.arange(token_count, dtype=jnp.int32)
    ancestor = jnp.sum((running[None, :] <= own_index[:, None]).astype(jnp.int32), axis=1)
    widened = padded(both_kv, ((("expert", "group"), 1),), REACH)
    window_index = first_index - REACH + jnp.arange(token_count + 2 * REACH, dtype=jnp.int32)
    selector = (ancestor[:, None] == window_index[None, :]).astype(jnp.bfloat16)
    resampled = jnp.einsum(
        "tw,kwhld->kthld", selector, widened, preferred_element_type=jnp.float32
    ).astype(jnp.bfloat16)
    return (layer_out, resampled[0], resampled[1])


def one_group_shards(
    hidden_in,
    queries,
    new_keys,
    new_values,
    cache_keys,
    cache_values,
    route_ids,
    route_weights,
    norm_gain,
    gate_weight,
    up_weight,
    down_weight,
    ancestor_counts,
):
    step_count, token_count, query_heads, head_width = queries.shape
    key_heads = cache_keys.shape[1]
    cached = cache_keys.shape[2]
    group_size = query_heads // key_heads
    rows = step_count * token_count
    model_width = hidden_in.shape[2]
    expert_count = lax.axis_size("expert")
    expert_index = lax.axis_index("expert")
    expert_local = gate_weight.shape[0]
    experts_all = expert_local * expert_count
    column_width = down_weight.shape[2]
    tensor_index = lax.axis_index("tensor")
    cache_pair = jnp.stack([cache_keys, cache_values])
    fresh_pair = jnp.transpose(jnp.stack([new_keys, new_values]), (0, 2, 3, 1, 4))
    both_kv = jnp.concatenate([cache_pair, fresh_pair], axis=3)
    length = both_kv.shape[3]
    grouped = queries.reshape(step_count, token_count, key_heads, group_size, head_width)
    scores = jnp.einsum(
        "sphgd,phld->sphgl", grouped, both_kv[0], preferred_element_type=jnp.float32
    ) / math.sqrt(head_width)
    allowed = lax.broadcasted_iota(
        jnp.int32, (step_count, length), 1
    ) <= cached + lax.broadcasted_iota(jnp.int32, (step_count, length), 0)
    scores = jnp.where(allowed[:, None, None, None, :], scores, -1e30)
    exponent = jnp.exp(scores - jnp.max(scores, axis=-1, keepdims=True))
    attn_weights = (exponent / jnp.sum(exponent, axis=-1, keepdims=True)).astype(jnp.bfloat16)
    attended = jnp.einsum(
        "sphgl,phld->sphgd", attn_weights, both_kv[1], preferred_element_type=jnp.float32
    )
    attended = attended.astype(jnp.bfloat16).reshape(rows, query_heads * head_width)
    attended = lax.all_gather(attended, "tensor", axis=1, tiled=True)
    residual = hidden_in.reshape(rows, model_width).astype(jnp.float32) + attended.astype(
        jnp.float32
    )
    normed = (
        residual
        * lax.rsqrt(jnp.mean(residual * residual, axis=-1, keepdims=True) + epsilon)
        * norm_gain
    ).astype(jnp.bfloat16)
    share = route_weights / jnp.sum(route_weights, axis=-1, keepdims=True)
    hits = route_ids[..., None] == jnp.arange(experts_all, dtype=jnp.int32)
    mix = jnp.sum(jnp.where(hits, share[..., None], 0.0), axis=2).reshape(rows, experts_all)
    counts = jnp.broadcast_to(ancestor_counts.astype(jnp.float32)[None, :], (rows, token_count))
    table = jnp.concatenate([mix, counts], axis=1)
    spare = -table.shape[1] % 128
    table = jnp.pad(table, ((0, 0), (0, spare)))
    table = lax.all_gather(table, "expert", axis=0, tiled=True)
    tokens = lax.all_gather(normed, "expert", axis=0, tiled=True)
    gate = jnp.einsum("ri,eif->erf", tokens, gate_weight, preferred_element_type=jnp.float32)
    up = jnp.einsum("ri,eif->erf", tokens, up_weight, preferred_element_type=jnp.float32)
    gate = gate.astype(jnp.bfloat16).astype(jnp.float32)
    up = up.astype(jnp.bfloat16).astype(jnp.float32)
    hidden = (jax.nn.silu(gate) * up).astype(jnp.bfloat16)
    hidden = lax.all_gather(hidden, "tensor", axis=2, tiled=True)
    answered = jnp.einsum("erf,efo->ero", hidden, down_weight, preferred_element_type=jnp.float32)
    own_mix = lax.dynamic_slice_in_dim(table, expert_index * expert_local, expert_local, axis=1)
    partial = jnp.sum(answered * own_mix.T[:, :, None], axis=0).astype(jnp.bfloat16)
    returned = lax.all_to_all(
        partial.reshape(expert_count, rows, column_width), "expert", 0, 0, tiled=True
    )
    expert_mix = jnp.sum(returned.astype(jnp.float32), axis=0)
    own_columns = lax.dynamic_slice_in_dim(
        residual, tensor_index * column_width, column_width, axis=1
    )
    half = (own_columns + expert_mix).astype(jnp.bfloat16)
    layer_out = lax.all_gather(half, "tensor", axis=1, tiled=True).reshape(
        step_count, token_count, model_width
    )
    every_count = table.reshape(expert_count, rows, -1)[
        :, 0, experts_all : experts_all + token_count
    ].reshape(-1)
    running = jnp.cumsum(every_count.astype(jnp.int32))
    first_index = expert_index * token_count
    own_index = first_index + jnp.arange(token_count, dtype=jnp.int32)
    ancestor = jnp.sum((running[None, :] <= own_index[:, None]).astype(jnp.int32), axis=1)
    widened = padded(both_kv, ((("expert", "group"), 1),), REACH)
    window_index = first_index - REACH + jnp.arange(token_count + 2 * REACH, dtype=jnp.int32)
    selector = (ancestor[:, None] == window_index[None, :]).astype(jnp.bfloat16)
    resampled = jnp.einsum(
        "tw,kwhld->kthld", selector, widened, preferred_element_type=jnp.float32
    ).astype(jnp.bfloat16)
    return (layer_out, resampled[0], resampled[1])


def solution(mesh):
    shards = one_group_shards if mesh.shape["group"] == 1 else grouped_shards
    in_specs = (
        P(None, ("parts", "expert", "group"), None),
        P(None, ("parts", "expert", "group"), "tensor", None),
        P(None, ("parts", "expert", "group"), "tensor", None),
        P(None, ("parts", "expert", "group"), "tensor", None),
        P(("parts", "expert", "group"), "tensor", None, None),
        P(("parts", "expert", "group"), "tensor", None, None),
        P(None, ("parts", "expert", "group"), None),
        P(None, ("parts", "expert", "group"), None),
        P(),
        P("expert", "group", "tensor"),
        P("expert", "group", "tensor"),
        P("expert", None, ("group", "tensor")),
        P(("parts", "expert", "group")),
    )
    out_specs = (
        P(None, ("parts", "expert", "group"), None),
        P(("parts", "expert", "group"), "tensor", None, None),
        P(("parts", "expert", "group"), "tensor", None, None),
    )
    return jax.shard_map(shards, mesh=mesh, in_specs=in_specs, out_specs=out_specs, check_vma=False)
```

profile of v0, /device:TPU:0, one launch (start us, length us, event | category | flops | bytes accessed | tf_op | source)
XLA Modules:
  0.0 117.5 jit_solution(2115568042403816963)
XLA Ops:
  0.6 0.0 copy-start
  0.6 0.0 copy-start.8
  0.7 0.0 copy-start.7
  0.7 0.0 copy-start.6
  0.7 0.0 copy-start.3
  0.7 0.8 copy_bitcast_fusion
  1.5 1.1 pad_maximum_fusion.1
  2.6 0.9 fusion.25
  3.4 5.0 %collective-permute-start = (bf16[2,2,2,131,128]{4,3,2,1,0:T(8,128)(2,1)}, bf16[2,2,2,131,128]{4,3,2,1,0:T(8,128)(2,1)S(1)}, u32[]{:S(2)}, u32[]{:S(2)}) collective-permute-start(bf16[2,2,2,131,128]{4,3,2,1,0:T(8,128)(2,1)} %get-tuple-element.17), channel_id=1, source_target_pairs={{0,2},{2,4},{4,6},{6,8},{8,10},{10,12},{12,14},{1,3},{3,5},{5,7},{... | collective-permute-start | bytes 804872 | tf_op jit(solution)/shard_map/ppermute | solution.py:20
  8.4 1.3 %collective-permute-start.1 = (bf16[2,2,2,131,128]{4,3,2,1,0:T(8,128)(2,1)}, bf16[2,2,2,131,128]{4,3,2,1,0:T(8,128)(2,1)}, u32[]{:S(2)}, u32[]{:S(2)}) collective-permute-start(bf16[2,2,2,131,128]{4,3,2,1,0:T(8,128)(2,1)} %get-tuple-element.18), channel_id=1, source_target_pairs={{2,0},{4,2},{6,4},{8,6},{10,8},{12,10},{14,12},{3,1},{5,3},{7,5},{... | collective-permute-start | bytes 804872 | tf_op jit(solution)/shard_map/ppermute | solution.py:22
  9.7 0.0 copy-done.8
  9.8 0.1 iota_compare_fusion.1
  9.8 0.0 copy-done.7
  9.8 0.1 fusion.20
  9.9 0.0 copy-done.6
  9.9 0.1 select_reduce_fusion
  10.1 0.1 pad.11.clone
  10.2 36.5 %all-gather.1 = f32[8,12,128]{2,1,0:T(8,128)S(1)} all-gather(f32[1,12,128]{2,1,0:T(8,128)S(1)} %pad_bitcast_fusion), channel_id=1, replica_groups=mesh['parts'=2,'expert'=8,'group'=1,'tensor'=2] {'expert'}, dimensions={0}, use_global_device_ids=true | all-gather | bytes 55296 | tf_op jit(solution)/shard_map/all_gather | solution.py:233
  46.6 0.1 dynamic-slice_bitcast_fusion
  46.7 0.6 copy.46
  47.4 0.0 copy-done.3
  47.4 0.0 copy-done
  47.4 0.3 fusion.11
  47.6 0.2 fusion.26
  47.9 0.4 fusion.13
  48.3 0.1 reshape.97
  48.3 1.9 %all_gather.15 = bf16[12,4096]{1,0:T(8,128)(2,1)S(1)} all-gather(bf16[12,2048]{1,0:T(8,128)(2,1)S(1)} %reshape.97), channel_id=1, replica_groups=mesh['parts'=2,'expert'=8,'group'=1,'tensor'=2] {'tensor'}, dimensions={1}, use_global_device_ids=true | all-gather | bytes 147456 | tf_op jit(solution)/shard_map/all_gather | solution.py:217
  50.2 0.2 multiply_reduce_fusion
  50.4 0.0 copy-done.4
  50.4 0.1 fusion.15
  50.5 34.9 %all-gather = bf16[8,12,4096]{2,1,0:T(8,128)(2,1)} all-gather(bf16[1,12,4096]{2,1,0:T(8,128)(2,1)S(1)} %fusion.15), channel_id=1, replica_groups=mesh['parts'=2,'expert'=8,'group'=1,'tensor'=2] {'expert'}, dimensions={0}, use_global_device_ids=true | all-gather | bytes 884736 | tf_op jit(solution)/shard_map/all_gather | solution.py:234
  85.4 1.5 %reshape.110 = bf16[96,4096,1]{1,0,2:T(8,128)(2,1)S(1)} reshape(bf16[8,12,4096]{2,1,0:T(8,128)(2,1)} %all-gather) | data formatting | bytes 1572864
  86.9 0.0 slice-start.1
  86.9 0.0 slice-start.2
  86.9 4.1 %fusion.9 = f32[2,96,384]{2,1,0:T(8,128)S(1)} fusion(bf16[96,4096,1]{1,0,2:T(8,128)(2,1)S(1)} %reshape.110, bf16[2,4096,384]{2,1,0:T(8,128)(2,1)} %param.22), kind=kOutput, calls=%fused_computation.13 | convolution fusion | flops 604127232 | bytes 7372800 | tf_op jit(solution)/shard_map/ri,eif->erf/dot_general | solution.py:235
  91.0 0.0 slice-done.1
  91.0 0.0 slice-start.3
  91.0 0.0 copy-start.5
  91.1 1.1 fusion.7
  92.2 2.0 %all_gather.17 = bf16[2,96,768]{2,1,0:T(8,128)(2,1)S(1)} all-gather(bf16[2,96,384]{2,1,0:T(8,128)(2,1)S(1)} %fusion.7), channel_id=1, replica_groups=mesh['parts'=2,'expert'=8,'group'=1,'tensor'=2] {'tensor'}, dimensions={2}, use_global_device_ids=true | all-gather | bytes 442368 | tf_op jit(solution)/shard_map/all_gather | solution.py:240
  94.2 0.0 slice-done.2
  94.2 1.2 fusion.1
  95.4 0.0 copy-start.1
  95.4 0.0 copy-start.2
  95.4 0.9 convert_element_type.103
  96.3 3.5 %all-to-all-start = ((bf16[8,12,2048]{2,1,0:T(8,128)(2,1)}), bf16[8,12,2048]{2,1,0:T(8,128)(2,1)S(1)}, u32[]{:S(2)}, u32[]{:S(2)}) async-start(bf16[8,12,2048]{2,1,0:T(8,128)(2,1)} %convert_element_type.103), calls=%async_computation | async-start | bytes 1048576 | tf_op jit(solution)/shard_map/all_to_all | solution.py:244
  99.8 0.1 fusion.18
  99.9 0.1 convert_element_type.114
  100.0 0.1 reduce-window.8
  100.0 0.1 reduce.1
  100.1 0.2 convert_reduce_fusion.1
  100.3 0.0 collective-permute-done
  100.4 0.0 collective-permute-done.1
  100.4 0.0 copy-done.1
  100.4 0.0 copy-done.2
  100.4 1.0 pad_maximum_fusion
  101.4 0.5 fusion.2
  101.9 0.2 slice_bitcast_fusion.4
  102.1 0.9 copy.50
  103.0 0.9 copy.49
  104.0 10.8 %all-to-all-done = bf16[8,12,2048]{2,1,0:T(8,128)(2,1)S(1)} async-done(((bf16[8,12,2048]{2,1,0:T(8,128)(2,1)}), bf16[8,12,2048]{2,1,0:T(8,128)(2,1)S(1)}, u32[]{:S(2)}, u32[]{:S(2)}) %all-to-all-start) | async-done | bytes 393248 | tf_op jit(solution)/shard_map/all_to_all | solution.py:244
  114.8 0.1 convert_reduce_fusion
  114.9 1.9 %all_gather.19 = bf16[12,4096]{1,0:T(8,128)(2,1)S(1)} all-gather(bf16[12,2048]{1,0:T(8,128)(2,1)S(1)} %add_convert_fusion), channel_id=1, replica_groups=mesh['parts'=2,'expert'=8,'group'=1,'tensor'=2] {'tensor'}, dimensions={1}, use_global_device_ids=true | all-gather | bytes 147456 | tf_op jit(solution)/shard_map/all_gather | solution.py:252
  116.8 0.7 reshape.99
  (20 shorter events, 0.1 us)
Async XLA Ops:
  0.6 46.7 %copy-start = (bf16[3,4,16,128]{3,2,1,0:T(8,128)(2,1)S(1)}, bf16[3,4,16,128]{3,2,1,0:T(8,128)(2,1)}, u32[]{:S(2)}) copy-start(bf16[3,4,16,128]{3,2,1,0:T(8,128)(2,1)} %param.14) | copy-start | bytes 147460
  0.6 9.1 %copy-start.8 = (s32[4]{0:T(128)S(1)}, s32[4]{0:T(128)}, u32[]{:S(2)}) copy-start(s32[4]{0:T(128)} %param.25) | copy-start | bytes 52
  0.7 9.2 %copy-start.7 = (f32[3,4,8]{2,1,0:T(4,128)S(1)}, f32[3,4,8]{2,1,0:T(4,128)}, u32[]{:S(2)}) copy-start(f32[3,4,8]{2,1,0:T(4,128)} %param.20) | copy-start | bytes 1156
  0.7 9.3 %copy-start.6 = (s32[3,4,8]{2,1,0:T(4,128)S(1)}, s32[3,4,8]{2,1,0:T(4,128)}, u32[]{:S(2)}) copy-start(s32[3,4,8]{2,1,0:T(4,128)} %param.19) | copy-start | bytes 1156
  0.7 46.7 %copy-start.3 = (bf16[3,4,4096]{2,1,0:T(4,128)(2,1)S(1)}, bf16[3,4,4096]{2,1,0:T(4,128)(2,1)}, u32[]{:S(2)}) copy-start(bf16[3,4,4096]{2,1,0:T(4,128)(2,1)} %param.13) | copy-start | bytes 294916
  3.4 47.0 %copy-start.4 = (f32[4096]{0:T(1024)S(1)}, f32[4096]{0:T(1024)}, u32[]{:S(2)}) copy-start(f32[4096]{0:T(1024)} %param.21) | copy-start | bytes 49156
  3.4 96.9 %collective-permute-start = (bf16[2,2,2,131,128]{4,3,2,1,0:T(8,128)(2,1)}, bf16[2,2,2,131,128]{4,3,2,1,0:T(8,128)(2,1)S(1)}, u32[]{:S(2)}, u32[]{:S(2)}) collective-permute-start(bf16[2,2,2,131,128]{4,3,2,1,0:T(8,128)(2,1)} %get-tuple-element.17), channel_id=1, source_target_pairs={{0,2},{2,4},{4,6},{6,8},{8,10},{10,12},{12,14},{1,3},{3,5},{5,7},{... | collective-permute-start | bytes 804872 | tf_op jit(solution)/shard_map/ppermute | solution.py:20
  8.4 91.9 %collective-permute-start.1 = (bf16[2,2,2,131,128]{4,3,2,1,0:T(8,128)(2,1)}, bf16[2,2,2,131,128]{4,3,2,1,0:T(8,128)(2,1)}, u32[]{:S(2)}, u32[]{:S(2)}) collective-permute-start(bf16[2,2,2,131,128]{4,3,2,1,0:T(8,128)(2,1)} %get-tuple-element.18), channel_id=1, source_target_pairs={{2,0},{4,2},{6,4},{8,6},{10,8},{12,10},{14,12},{3,1},{5,3},{7,5},{... | collective-permute-start | bytes 804872 | tf_op jit(solution)/shard_map/ppermute | solution.py:22
  85.4 5.6 %slice-start = ((s8[6291456]{0:T(1024)(128)(4,1)}), s8[2097152]{0:T(1024)(128)(4,1)S(1)}, s32[]{:S(2)}) async-start(s8[6291456]{0:T(1024)(128)(4,1)} %bitcast.66), calls=%async_computation.1 | async-start | bytes 4194304
  86.9 4.1 %slice-start.1 = ((s8[6291456]{0:T(1024)(128)(4,1)}), s8[4194304]{0:T(1024)(128)(4,1)S(1)}, s32[]{:S(2)}) async-start(s8[6291456]{0:T(1024)(128)(4,1)} %bitcast.66), calls=%async_computation.2 | async-start | bytes 8388608
  86.9 7.3 %slice-start.2 = ((s8[6291456]{0:T(1024)(128)(4,1)}), s8[4194304]{0:T(1024)(128)(4,1)S(1)}, s32[]{:S(2)}) async-start(s8[6291456]{0:T(1024)(128)(4,1)} %bitcast.68), calls=%async_computation.3 | async-start | bytes 8388608
  91.0 3.2 %slice-start.3 = ((s8[6291456]{0:T(1024)(128)(4,1)}), s8[2097152]{0:T(1024)(128)(4,1)S(1)}, s32[]{:S(2)}) async-start(s8[6291456]{0:T(1024)(128)(4,1)} %bitcast.68), calls=%async_computation.4 | async-start | bytes 4194304
  91.0 3.2 %copy-start.5 = (f32[2,96]{1,0:T(2,128)S(1)}, f32[2,96]{1,0:T(2,128)}, u32[]{:S(2)}) copy-start(f32[2,96]{1,0:T(2,128)} %copy.46) | copy-start | bytes 2308
  95.4 5.0 %copy-start.1 = (bf16[4,2,128,128]{3,2,1,0:T(8,128)(2,1)S(1)}, bf16[4,2,128,128]{3,2,1,0:T(8,128)(2,1)}, u32[]{:S(2)}) copy-start(bf16[4,2,128,128]{3,2,1,0:T(8,128)(2,1)} %param.18) | copy-start | bytes 786436
  95.4 5.0 %copy-start.2 = (bf16[4,2,128,128]{3,2,1,0:T(8,128)(2,1)S(1)}, bf16[4,2,128,128]{3,2,1,0:T(8,128)(2,1)}, u32[]{:S(2)}) copy-start(bf16[4,2,128,128]{3,2,1,0:T(8,128)(2,1)} %param.17) | copy-start | bytes 786436
  96.3 18.5 %all-to-all-start = ((bf16[8,12,2048]{2,1,0:T(8,128)(2,1)}), bf16[8,12,2048]{2,1,0:T(8,128)(2,1)S(1)}, u32[]{:S(2)}, u32[]{:S(2)}) async-start(bf16[8,12,2048]{2,1,0:T(8,128)(2,1)} %convert_element_type.103), calls=%async_computation | async-start | bytes 1048576 | tf_op jit(solution)/shard_map/all_to_all | solution.py:244
where the time goes:
time: 118 us; the launch traced here: 117 us
  blocking collectives  77.2 us (65%)
  waiting for transfers between devices  10.8 us (9%)
  starting transfers between devices  9.79 us (8%)
  local copies, waits for them, and re-layouts  7.75 us (7%)
  matrix products  7.53 us (6%)
  other arithmetic  3.44 us (3%)
    all_gather x1, blocking collectives, one_group_shards(): table = lax.all_gather(table, 'expert', axis=0, tiled=True)  36.5 us
    all_gather x1, blocking collectives, one_group_shards(): tokens = lax.all_gather(normed, 'expert', axis=0, tiled=True)  34.9 us
    all_to_all x1, waiting for transfers between devices, one_group_shards(): lax.all_to_all(partial.reshape(expert_count, rows, column_width), 'expert...  10.8 us
    ppermute x1, starting transfers between devices, padded(): lax.ppermute(tail, axis, [(i, (i + 1) % count) for i in range(ends)])  5.01 us
    dot_general x1, matrix products, one_group_shards(): jnp.einsum('ri,eif->erf', tokens, gate_weight, preferred_element_type=jnp...  4.06 us
    all_to_all x1, starting transfers between devices, one_group_shards(): lax.all_to_all(partial.reshape(expert_count, rows, column_width), 'expert...  3.49 us
    unnamed x31, local copies, waits for them, and re-layouts  3.42 us
  transfers between devices with their start and end apart: 3, of which 1 were waited for; matrix products, arithmetic and copies ran while one was open for 13% of the time, Pallas kernels for 0%

commit v1 on v0

--- a/solution.py
+++ b/solution.py
@@ -230,8 +230,11 @@
     table = jnp.concatenate([mix, counts], axis=1)
     spare = -table.shape[1] % 128
     table = jnp.pad(table, ((0, 0), (0, spare)))
-    table = lax.all_gather(table, "expert", axis=0, tiled=True)
-    tokens = lax.all_gather(normed, "expert", axis=0, tiled=True)
+    table, tokens = jnp.split(
+        lax.all_gather(jnp.concatenate([table, normed], 1), axis=0, tiled=True, axis_name="expert"),
+        [table.shape[1]],
+        axis=1,
+    )
     gate = jnp.einsum("ri,eif->erf", tokens, gate_weight, preferred_element_type=jnp.float32)
     up = jnp.einsum("ri,eif->erf", tokens, up_weight, preferred_element_type=jnp.float32)
     gate = gate.astype(jnp.bfloat16).astype(jnp.float32)

time: 118 us -> 115 us (0.975)
  blocking collectives: 77.2 us -> 5.96 us
  waiting for transfers between devices: 10.8 us -> 62 us
  between operations: 0.98 us -> 14.3 us
  matrix products: 7.53 us -> 13 us
  local copies, waits for them, and re-layouts: 7.75 us -> 6.43 us
    all_gather x2 -> x0, blocking collectives: 71.3 us -> none  [the longest x1 36.5 us: one_group_shards(): table = lax.all_gather(table, 'expert', axis=0, tiled=True)]
    all_gather x0 -> x1, waiting for transfers between devices: none -> 37 us  [one_group_shards(): lax.all_gather(jnp.concatenate([table, normed], 1), axis=0, tiled=True, a...]
    ppermute x1, waiting for transfers between devices: 0.01 us -> 13.1 us  [padded(): lax.ppermute(tail, axis, [(i, (i + 1) % count) for i in range(ends)])]
    dot_general x1, matrix products: 1.16 us -> 3.98 us  [one_group_shards(): jnp.einsum('erf,efo->ero', hidden, down_weight, preferred_element_type=jn...]
    dot_general x1, matrix products: 1.14 us -> 3.93 us  [one_group_shards(): jnp.einsum('ri,eif->erf', tokens, up_weight, preferred_element_type=jnp.f...]
    unnamed x31 -> x19, local copies, waits for them, and re-layouts: 3.42 us -> 3.53 us
  transfers between devices with their start and end apart: 3 -> 4, of which waited for: 1 -> 3; matrix products, arithmetic and copies ran while one was open for 13% -> 3% of each run, Pallas kernels for 0% -> 0%
where the time goes in v1:
time: 115 us
  waiting for transfers between devices  62 us (54%)
  between operations  14.3 us (12%)
  matrix products  13 us (11%)
  starting transfers between devices  9.57 us (8%)
  local copies, waits for them, and re-layouts  6.43 us (6%)
  blocking collectives  5.96 us (5%)
  other arithmetic  3.25 us (3%)
    all_gather x1, waiting for transfers between devices, one_group_shards(): lax.all_gather(jnp.concatenate([table, normed], 1), axis=0, tiled=True, a...  37 us
    ppermute x1, waiting for transfers between devices, padded(): lax.ppermute(tail, axis, [(i, (i + 1) % count) for i in range(ends)])  13.1 us
    all_to_all x1, waiting for transfers between devices, one_group_shards(): lax.all_to_all(partial.reshape(expert_count, rows, column_width), 'expert...  11.9 us
    ppermute x1, starting transfers between devices, padded(): lax.ppermute(tail, axis, [(i, (i + 1) % count) for i in range(ends)])  4.75 us
    dot_general x1, matrix products, one_group_shards(): jnp.einsum('erf,efo->ero', hidden, down_weight, preferred_element_type=jn...  3.98 us
    dot_general x1, matrix products, one_group_shards(): jnp.einsum('ri,eif->erf', tokens, up_weight, preferred_element_type=jnp.f...  3.93 us
    dot_general x1, matrix products, one_group_shards(): jnp.einsum('ri,eif->erf', tokens, gate_weight, preferred_element_type=jnp...  3.91 us
    unnamed x19, local copies, waits for them, and re-layouts  3.53 us
  transfers between devices with their start and end apart: 4, of which 3 were waited for; matrix products, arithmetic and copies ran while one was open for 3% of the time, Pallas kernels for 0%

profile of v1, /device:TPU:0, one launch (start us, length us, event | category | flops | bytes accessed | tf_op | source)
XLA Modules:
  0.0 114.6 jit_solution(5811231508816310243)
XLA Ops:
  7.2 0.0 copy-start
  7.2 0.0 all-gather.3.cloned.1.call-start
  7.2 0.1 iota_compare_fusion.2
  7.3 0.7 copy_bitcast_fusion
  8.0 0.0 copy-start.3
  8.1 1.1 pad_maximum_fusion.1
  9.2 0.0 copy-done
  9.2 0.0 copy-start.6
  9.2 0.3 fusion.15
  9.5 0.0 copy-start.5
  9.5 0.0 copy-start.7
  9.5 0.0 copy-start.4
  9.5 0.2 fusion.31
  9.7 0.4 fusion.17
  10.1 0.1 reshape.97
  10.2 2.0 %all_gather.12 = bf16[12,4096]{1,0:T(8,128)(2,1)S(1)} all-gather(bf16[12,2048]{1,0:T(8,128)(2,1)S(1)} %reshape.97), channel_id=1, replica_groups=mesh['parts'=2,'expert'=8,'group'=1,'tensor'=2] {'tensor'}, dimensions={1}, use_global_device_ids=true | all-gather | bytes 147456 | tf_op jit(solution)/shard_map/all_gather | solution.py:217
  12.2 0.0 copy-done.3
  12.2 0.0 copy-start.1
  12.3 0.0 copy-start.2
  12.3 0.2 multiply_reduce_fusion
  12.4 0.0 copy-done.6
  12.4 0.1 fusion.25
  12.5 0.0 copy-done.5
  12.5 0.1 select_reduce_fusion
  12.7 0.0 copy-done.7
  12.7 0.1 pad.13.clone
  12.8 0.0 copy-done.4
  12.8 0.1 fusion.20
  12.9 0.7 fusion.19
  13.6 0.0 all-gather.3.cloned.1.call-update
  13.7 4.8 %collective-permute-start = (bf16[2,2,2,131,128]{4,3,2,1,0:T(8,128)(2,1)S(1)}, bf16[2,2,2,131,128]{4,3,2,1,0:T(8,128)(2,1)S(1)}, u32[]{:S(2)}, u32[]{:S(2)}) collective-permute-start(bf16[2,2,2,131,128]{4,3,2,1,0:T(8,128)(2,1)S(1)} %get-tuple-element.17), channel_id=1, source_target_pairs={{0,2},{2,4},{4,6},{6,8},{8,10},{10,12},{12,14},{1,3},{3,5},{5,7},{... | collective-permute-start | bytes 804872 | tf_op jit(solution)/shard_map/ppermute | solution.py:20
  18.4 1.3 %collective-permute-start.1 = (bf16[2,2,2,131,128]{4,3,2,1,0:T(8,128)(2,1)S(1)}, bf16[2,2,2,131,128]{4,3,2,1,0:T(8,128)(2,1)S(1)}, u32[]{:S(2)}, u32[]{:S(2)}) collective-permute-start(bf16[2,2,2,131,128]{4,3,2,1,0:T(8,128)(2,1)S(1)} %get-tuple-element.18), channel_id=1, source_target_pairs={{2,0},{4,2},{6,4},{8,6},{10,8},{12,10},{14,12},{3,1},{5,3},{7,5},{... | collective-permute-start | bytes 804872 | tf_op jit(solution)/shard_map/ppermute | solution.py:22
  19.8 13.1 %collective-permute-done = bf16[2,2,2,131,128]{4,3,2,1,0:T(8,128)(2,1)S(1)} collective-permute-done((bf16[2,2,2,131,128]{4,3,2,1,0:T(8,128)(2,1)S(1)}, bf16[2,2,2,131,128]{4,3,2,1,0:T(8,128)(2,1)S(1)}, u32[]{:S(2)}, u32[]{:S(2)}) %collective-permute-start) | collective-permute-done | bytes 268320 | tf_op jit(solution)/shard_map/ppermute | solution.py:20
  32.9 0.0 collective-permute-done.1
  32.9 0.0 copy-done.1
  32.9 0.0 copy-done.2
  32.9 0.1 pad_maximum_fusion
  33.0 37.0 %all-gather.3.cloned.1.call-done = f32[8,12,4224]{2,1,0:T(8,128)} async-done(((f32[1,12,4224]{2,1,0:T(8,128)}), f32[8,12,4224]{2,1,0:T(8,128)}) %all-gather.3.cloned.1.call-update) | async-done | bytes 1622032 | tf_op jit(solution)/shard_map/all_gather | solution.py:234
  70.0 1.7 %reshape.104 = f32[96,4224]{1,0:T(8,128)S(1)} reshape(f32[8,12,4224]{2,1,0:T(8,128)} %all-gather.3.cloned.1.call-done) | data formatting | bytes 3244032
  71.6 3.9 %fusion.8 = f32[2,96,384]{2,1,0:T(8,128)S(1)} fusion(bf16[2,4096,384]{2,1,0:T(8,128)(2,1)} %param.22, f32[96,4224]{1,0:T(8,128)S(1)} %reshape.104), kind=kOutput, calls=%fused_computation.11 | convolution fusion | flops 604053504 | bytes 7372800 | tf_op jit(solution)/shard_map/ri,eif->erf/dot_general | solution.py:238
  75.5 3.9 %fusion.13 = bf16[2,96,384]{2,1,0:T(8,128)(2,1)S(1)} fusion(bf16[2,4096,384]{2,1,0:T(8,128)(2,1)} %param.23, f32[96,4224]{1,0:T(8,128)S(1)} %reshape.104, f32[2,96,384]{2,1,0:T(8,128)S(1)} %fusion.8), kind=kOutput, calls=%fused_computation.16 | convolution fusion | flops 604495872 | bytes 7520256 | tf_op jit(solution)/shard_map/ri,eif->erf/dot_general | solution.py:239
  79.5 2.0 %all_gather.14 = bf16[2,96,768]{2,1,0:T(8,128)(2,1)S(1)} all-gather(bf16[2,96,384]{2,1,0:T(8,128)(2,1)S(1)} %fusion.13), channel_id=1, replica_groups=mesh['parts'=2,'expert'=8,'group'=1,'tensor'=2] {'tensor'}, dimensions={2}, use_global_device_ids=true | all-gather | bytes 442368 | tf_op jit(solution)/shard_map/all_gather | solution.py:243
  81.5 0.1 dynamic-slice_bitcast_fusion
  81.6 0.1 copy.47
  81.6 4.0 %fusion.1 = bf16[96,2048]{1,0:T(8,128)(2,1)S(1)} fusion(bf16[2,96,768]{2,1,0:T(8,128)(2,1)S(1)} %all_gather.14, bf16[2,768,2048]{2,1,0:T(8,128)(2,1)} %param.24, f32[2,96]{1,0:T(2,128)S(1)} %copy.47), kind=kOutput, calls=%fused_computation.3 | convolution fusion | flops 604569600 | bytes 6980352 | tf_op jit(solution)/shard_map/erf,efo->ero/dot_general | solution.py:244
  85.6 0.9 convert_element_type.107
  86.5 3.5 %all-to-all-start = ((bf16[8,12,2048]{2,1,0:T(8,128)(2,1)}), bf16[8,12,2048]{2,1,0:T(8,128)(2,1)S(1)}, u32[]{:S(2)}, u32[]{:S(2)}) async-start(bf16[8,12,2048]{2,1,0:T(8,128)(2,1)} %convert_element_type.107), calls=%async_computation | async-start | bytes 1048576 | tf_op jit(solution)/shard_map/all_to_all | solution.py:247
  90.0 0.1 fusion.23
  90.1 0.1 convert_element_type.118
  90.2 0.1 reduce-window.8
  90.2 0.1 reduce.1
  90.3 0.2 convert_reduce_fusion.1
  90.5 0.5 fusion.4
  91.0 0.2 slice_bitcast_fusion.23
  91.2 0.9 copy.50
  92.2 0.9 copy.51
  93.1 11.9 %all-to-all-done = bf16[8,12,2048]{2,1,0:T(8,128)(2,1)S(1)} async-done(((bf16[8,12,2048]{2,1,0:T(8,128)(2,1)}), bf16[8,12,2048]{2,1,0:T(8,128)(2,1)S(1)}, u32[]{:S(2)}, u32[]{:S(2)}) %all-to-all-start) | async-done | bytes 393248 | tf_op jit(solution)/shard_map/all_to_all | solution.py:247
  105.0 0.1 convert_reduce_fusion
  105.1 1.9 %all_gather.15 = bf16[12,4096]{1,0:T(8,128)(2,1)S(1)} all-gather(bf16[12,2048]{1,0:T(8,128)(2,1)S(1)} %add_convert_fusion), channel_id=1, replica_groups=mesh['parts'=2,'expert'=8,'group'=1,'tensor'=2] {'tensor'}, dimensions={1}, use_global_device_ids=true | all-gather | bytes 147456 | tf_op jit(solution)/shard_map/all_gather | solution.py:255
  107.0 0.7 reshape.99
  (14 shorter events, 0.2 us)
Async XLA Ops:
  7.2 2.0 %copy-start = (bf16[3,4,16,128]{3,2,1,0:T(8,128)(2,1)S(1)}, bf16[3,4,16,128]{3,2,1,0:T(8,128)(2,1)}, u32[]{:S(2)}) copy-start(bf16[3,4,16,128]{3,2,1,0:T(8,128)(2,1)} %param.14) | copy-start | bytes 147460
  7.2 62.8 %all-gather.3.cloned.1.call-start = ((), (), s32[]{:S(2)}) async-start(), calls=%async_computation.1 | async-start | bytes 2433024 | tf_op jit(solution)/shard_map/all_gather | solution.py:234
  8.0 4.2 %copy-start.3 = (bf16[3,4,4096]{2,1,0:T(4,128)(2,1)S(1)}, bf16[3,4,4096]{2,1,0:T(4,128)(2,1)}, u32[]{:S(2)}) copy-start(bf16[3,4,4096]{2,1,0:T(4,128)(2,1)} %param.13) | copy-start | bytes 294916
  9.2 3.3 %copy-start.6 = (f32[3,4,8]{2,1,0:T(4,128)S(1)}, f32[3,4,8]{2,1,0:T(4,128)}, u32[]{:S(2)}) copy-start(f32[3,4,8]{2,1,0:T(4,128)} %param.20) | copy-start | bytes 1156
  9.5 3.1 %copy-start.5 = (s32[3,4,8]{2,1,0:T(4,128)S(1)}, s32[3,4,8]{2,1,0:T(4,128)}, u32[]{:S(2)}) copy-start(s32[3,4,8]{2,1,0:T(4,128)} %param.19) | copy-start | bytes 1156
  9.5 3.2 %copy-start.7 = (s32[4]{0:T(128)S(1)}, s32[4]{0:T(128)}, u32[]{:S(2)}) copy-start(s32[4]{0:T(128)} %param.25) | copy-start | bytes 52
  9.5 3.3 %copy-start.4 = (f32[4096]{0:T(1024)S(1)}, f32[4096]{0:T(1024)}, u32[]{:S(2)}) copy-start(f32[4096]{0:T(1024)} %param.21) | copy-start | bytes 49156
  12.2 20.7 %copy-start.1 = (bf16[4,2,128,128]{3,2,1,0:T(8,128)(2,1)S(1)}, bf16[4,2,128,128]{3,2,1,0:T(8,128)(2,1)}, u32[]{:S(2)}) copy-start(bf16[4,2,128,128]{3,2,1,0:T(8,128)(2,1)} %param.18) | copy-start | bytes 786436
  12.3 20.6 %copy-start.2 = (bf16[4,2,128,128]{3,2,1,0:T(8,128)(2,1)S(1)}, bf16[4,2,128,128]{3,2,1,0:T(8,128)(2,1)}, u32[]{:S(2)}) copy-start(bf16[4,2,128,128]{3,2,1,0:T(8,128)(2,1)} %param.17) | copy-start | bytes 786436
  13.7 19.2 %collective-permute-start = (bf16[2,2,2,131,128]{4,3,2,1,0:T(8,128)(2,1)S(1)}, bf16[2,2,2,131,128]{4,3,2,1,0:T(8,128)(2,1)S(1)}, u32[]{:S(2)}, u32[]{:S(2)}) collective-permute-start(bf16[2,2,2,131,128]{4,3,2,1,0:T(8,128)(2,1)S(1)} %get-tuple-element.17), channel_id=1, source_target_pairs={{0,2},{2,4},{4,6},{6,8},{8,10},{10,12},{12,14},{1,3},{3,5},{5,7},{... | collective-permute-start | bytes 804872 | tf_op jit(solution)/shard_map/ppermute | solution.py:20
  18.4 14.5 %collective-permute-start.1 = (bf16[2,2,2,131,128]{4,3,2,1,0:T(8,128)(2,1)S(1)}, bf16[2,2,2,131,128]{4,3,2,1,0:T(8,128)(2,1)S(1)}, u32[]{:S(2)}, u32[]{:S(2)}) collective-permute-start(bf16[2,2,2,131,128]{4,3,2,1,0:T(8,128)(2,1)S(1)} %get-tuple-element.18), channel_id=1, source_target_pairs={{2,0},{4,2},{6,4},{8,6},{10,8},{12,10},{14,12},{3,1},{5,3},{7,5},{... | collective-permute-start | bytes 804872 | tf_op jit(solution)/shard_map/ppermute | solution.py:22
  86.5 18.5 %all-to-all-start = ((bf16[8,12,2048]{2,1,0:T(8,128)(2,1)}), bf16[8,12,2048]{2,1,0:T(8,128)(2,1)S(1)}, u32[]{:S(2)}, u32[]{:S(2)}) async-start(bf16[8,12,2048]{2,1,0:T(8,128)(2,1)} %convert_element_type.107), calls=%async_computation | async-start | bytes 1048576 | tf_op jit(solution)/shard_map/all_to_all | solution.py:247
Sparse Core Ops, SparseCore 0:
  13.7 56.1 all-gather.2
